TPU v7x, 512 devices: a whole 4x8x8 slice. The times are simulated.
512 devices in a mesh: row: 8 (over z_lo, core), col: 8 (over x, z_hi), tm: 8 (over y).
Axes of the slice: x: 4, y: 8, z: 8 (z_hi: 2, z_lo: 4; z = z_hi * 4 + z_lo), core: 2. Of those that a mesh axis runs over, the one named last changes fastest.
Arguments:
- green_occ: bfloat16 [16, 256, 30720], P('tm', 'row', 'col'), may hold values from -6 to 6
- green_virt: bfloat16 [16, 256, 30720], P('tm', 'row', 'col'), may hold values from -6 to 6
- adjoint_w: bfloat16 [16, 256, 30720], P(None, 'row', ('col', 'tm')), may hold values from -6 to 6
- grad_basis: float32 [3, 256], P(None, 'row'), may hold values from -6 to 6
- owner_map: int32 [30720], replicated, may hold values from 0 to 999
- block_offset: int32 [8], P('row'), may hold values from 0 to 30688
Outputs:
- chi_freq: bfloat16 [16, 256, 30720], P(None, 'row', ('col', 'tm'))
- forces: float32 [3, 1000], replicated
All inputs are finite; a program needn't handle non-finite values.
Results may differ from a plain program's by a relative error of at most 0.0085.
Values may be sent and summed in bfloat16 or wider, within the bound.
No kernel may reach another device: no remote copies, remote signals or barrier semaphores. Data moves between devices by JAX's collectives and lax.ppermute only.
A program may use at most 64 MiB of HBM per device.

v0:
```python
import math
import jax
import jax.numpy as jnp
from jax import lax
from jax.sharding import PartitionSpec as P

NG = 30720
NTAU = 16
NATOM = 1000


def cos_table(count):
    steps = jnp.arange(count).astype(jnp.float32)
    tau = 0.1 * jnp.power(jnp.float32(1.35), steps)
    omega = 0.15 * jnp.power(jnp.float32(1.35), steps)
    return jnp.cos(omega[:, None] * tau[None, :]) / 4.0


def on_device(green_occ, green_virt, adjoint_w, grad_basis, owner_map, block_offset):
    table = cos_table(NTAU)
    scale = 1.0 / math.sqrt(NTAU * NG)
    row_count = green_occ.shape[1]
    product = (green_occ.astype(jnp.float32) * green_virt.astype(jnp.float32)).astype(jnp.bfloat16)
    chi_freq = jnp.einsum(
        "kt,tnc->knc",
        table,
        lax.all_to_all(product, "tm", split_axis=2, concat_axis=0, tiled=True).astype(jnp.float32),
        precision=lax.Precision.HIGHEST,
    ).astype(jnp.bfloat16)
    partial_value = (
        jnp.sum(adjoint_w.astype(jnp.float32) * chi_freq.astype(jnp.float32), axis=(0, 2)) * scale
    )
    owners = lax.dynamic_slice_in_dim(owner_map, block_offset[0], row_count, 0)
    onehot = (owners[:, None] == jnp.arange(NATOM)[None, :]).astype(jnp.float32)
    energy = lax.psum(partial_value, ("col", "tm"))
    local_forces = jnp.dot(
        grad_basis * energy[None, :],
        onehot,
        precision=lax.Precision.HIGHEST,
        preferred_element_type=jnp.float32,
    )
    forces = lax.psum(local_forces, "row")
    return (chi_freq, forces)


def solution(mesh):
    in_specs = (
        P("tm", "row", "col"),
        P("tm", "row", "col"),
        P(None, "row", ("col", "tm")),
        P(None, "row"),
        P(),
        P("row"),
    )
    out_specs = (P(None, "row", ("col", "tm")), P())
    return jax.shard_map(
        on_device, mesh=mesh, in_specs=in_specs, out_specs=out_specs, check_vma=False
    )
```

profile of v0, /device:TPU:1, one launch (start us, length us, event | category | flops | bytes accessed | tf_op | source)
XLA Modules:
  0.0 282.4 jit_solution(8296169190990714850)
XLA Ops:
  0.6 1.3 multiply_convert_fusion
  1.9 1.4 copy.16
  3.3 2.5 reshape.19
  5.9 7.7 %all-to-all-start = ((bf16[8,2,15360]{2,1,0:T(2,128)(2,1)}), bf16[8,2,15360]{2,1,0:T(2,128)(2,1)S(1)}, u32[]{:S(2)}, u32[]{:S(2)}) async-start(bf16[8,2,15360]{2,1,0:T(2,128)(2,1)} %reshape.19), calls=%async_computation | async-start | bytes 983040 | tf_op jit(solution)/shard_map/all_to_all | solution.py:27
  14.2 0.8 dynamic_slice.3
  15.0 12.4 %all-to-all-done = bf16[8,2,15360]{2,1,0:T(2,128)(2,1)S(1)} async-done(((bf16[8,2,15360]{2,1,0:T(2,128)(2,1)}), bf16[8,2,15360]{2,1,0:T(2,128)(2,1)S(1)}, u32[]{:S(2)}, u32[]{:S(2)}) %all-to-all-start) | async-done | bytes 491552 | tf_op jit(solution)/shard_map/all_to_all | solution.py:27
  27.4 1.0 reshape.20
  28.4 0.0 copy-start
  28.4 1.5 copy.17
  29.9 0.0 copy-start.1
  29.9 0.4 all_to_all.16
  30.3 0.0 copy-done
  30.4 1.1 multiply_reduce_fusion
  31.5 1.1 copy.19
  32.5 196.4 %psum.14 = f32[32]{0:T(128)S(1)} all-reduce(f32[32]{0:T(128)S(1)} %broadcast_multiply_fusion), channel_id=1, replica_groups=mesh['row'=8,'col'=8,'tm'=8] {'col','tm'}, use_global_device_ids=true, to_apply=%region_1.0 | all-reduce | flops 32 | bytes 256 | tf_op jit(solution)/shard_map/psum | solution.py:35
  228.9 0.0 copy-done.1
  228.9 0.2 fusion
  229.1 53.3 %psum.15 = f32[3,1000]{1,0:T(4,128)} all-reduce(f32[3,1000]{1,0:T(4,128)S(1)} %fusion), channel_id=1, replica_groups=mesh['row'=8,'col'=8,'tm'=8] {'row'}, use_global_device_ids=true, to_apply=%region_2.0 | all-reduce | flops 3000 | bytes 24000 | tf_op jit(solution)/shard_map/psum | solution.py:42
  (2 shorter events, 0.0 us)
Async XLA Ops:
  5.9 21.5 %all-to-all-start = ((bf16[8,2,15360]{2,1,0:T(2,128)(2,1)}), bf16[8,2,15360]{2,1,0:T(2,128)(2,1)S(1)}, u32[]{:S(2)}, u32[]{:S(2)}) async-start(bf16[8,2,15360]{2,1,0:T(2,128)(2,1)} %reshape.19), calls=%async_computation | async-start | bytes 983040 | tf_op jit(solution)/shard_map/all_to_all | solution.py:27
  28.4 2.0 copy-start
  29.9 199.0 %copy-start.1 = (f32[3,32]{1,0:T(4,128)S(1)}, f32[3,32]{1,0:T(4,128)}, u32[]{:S(2)}) copy-start(f32[3,32]{1,0:T(4,128)} %param.9) | copy-start | bytes 1156
where the time goes:
time: 283 us; the launch traced here: 282 us
  blocking collectives  250 us (88%)
  waiting for transfers between devices  12.4 us (4%)
  local copies, waits for them, and re-layouts  8.71 us (3%)
  starting transfers between devices  7.65 us (3%)
    psum x1, blocking collectives, on_device(): energy = lax.psum(partial_value, ('col', 'tm'))  196 us
    psum x1, blocking collectives, on_device(): forces = lax.psum(local_forces, 'row')  53.3 us
    all_to_all x1, waiting for transfers between devices, on_device(): lax.all_to_all(product, 'tm', split_axis=2, concat_axis=0, tiled=True)  12.4 us
    all_to_all x1, starting transfers between devices, on_device(): lax.all_to_all(product, 'tm', split_axis=2, concat_axis=0, tiled=True)  7.65 us
  transfers between devices with their start and end apart: 1, of which 1 were waited for; matrix products, arithmetic and copies ran while one was open for 0% of the time, Pallas kernels for 0%

commit v1 on v0

--- a/solution.py
+++ b/solution.py
@@ -32,7 +32,7 @@
     )
     owners = lax.dynamic_slice_in_dim(owner_map, block_offset[0], row_count, 0)
     onehot = (owners[:, None] == jnp.arange(NATOM)[None, :]).astype(jnp.float32)
-    energy = lax.psum(partial_value, ("col", "tm"))
+    energy = lax.psum(lax.psum(partial_value, "col"), "tm")
     local_forces = jnp.dot(
         grad_basis * energy[None, :],
         onehot,

time: 283 us -> 112 us (0.40)
  the two profiles are of different devices: /device:TPU:1 before, /device:TPU:8 now
where the time goes in v1:
time: 112 us; the launch traced here: 111 us
  blocking collectives  77.2 us (69%)
  waiting for transfers between devices  12.2 us (11%)
  starting transfers between devices  9.21 us (8%)
  local copies, waits for them, and re-layouts  8.71 us (8%)
  between operations  1.36 us (1%)
  matrix products  1.31 us (1%)
  other arithmetic  1.3 us (1%)
    psum x2, blocking collectives, on_device(): energy = lax.psum(lax.psum(partial_value, 'col'), 'tm')  50.7 us
    psum x1, blocking collectives, on_device(): forces = lax.psum(local_forces, 'row')  26.5 us
    all_to_all x1, waiting for transfers between devices, on_device(): lax.all_to_all(product, 'tm', split_axis=2, concat_axis=0, tiled=True)  12.2 us
    all_to_all x1, starting transfers between devices, on_device(): lax.all_to_all(product, 'tm', split_axis=2, concat_axis=0, tiled=True)  9.21 us
    unnamed x7, local copies, waits for them, and re-layouts  4.61 us
  transfers between devices with their start and end apart: 1, of which 1 were waited for; matrix products, arithmetic and copies ran while one was open for 1% of the time, Pallas kernels for 0%

profile of v1, /device:TPU:8, one launch (start us, length us, event | category | flops | bytes accessed | tf_op | source)
XLA Modules:
  0.0 111.3 jit_solution(6028683147570743248)
XLA Ops:
  0.6 1.3 %multiply_convert_fusion = bf16[2,32,3840]{2,1,0:T(8,128)(2,1)S(1)} fusion(bf16[2,32,3840]{2,1,0:T(8,128)(2,1)} %param.7, bf16[2,32,3840]{2,1,0:T(8,128)(2,1)} %param.6), kind=kLoop, calls=%fused_computation.2 | loop fusion | flops 983040 | bytes 1474560 | tf_op jit(solution)/shard_map/convert_element_type | solution.py:23
  1.9 1.4 %copy.16 = bf16[2,32,3840]{1,0,2:T(2,128)(2,1)S(1)} copy(bf16[2,32,3840]{2,1,0:T(8,128)(2,1)S(1)} %multiply_convert_fusion) | data formatting | bytes 983040 | tf_op jit(solution)/shard_map/convert_element_type | solution.py:23
  3.3 2.5 %reshape.19 = bf16[8,2,15360]{2,1,0:T(2,128)(2,1)} reshape(bf16[3840,2,32]{2,1,0:T(2,128)(2,1)S(1)} %bitcast.16) | data formatting | bytes 983040
  5.9 9.2 %all-to-all-start = ((bf16[8,2,15360]{2,1,0:T(2,128)(2,1)}), bf16[8,2,15360]{2,1,0:T(2,128)(2,1)S(1)}, u32[]{:S(2)}, u32[]{:S(2)}) async-start(bf16[8,2,15360]{2,1,0:T(2,128)(2,1)} %reshape.19), calls=%async_computation | async-start | bytes 983040 | tf_op jit(solution)/shard_map/all_to_all | solution.py:27
  15.7 0.8 dynamic_slice.3
  16.5 12.2 %all-to-all-done = bf16[8,2,15360]{2,1,0:T(2,128)(2,1)S(1)} async-done(((bf16[8,2,15360]{2,1,0:T(2,128)(2,1)}), bf16[8,2,15360]{2,1,0:T(2,128)(2,1)S(1)}, u32[]{:S(2)}, u32[]{:S(2)}) %all-to-all-start) | async-done | bytes 491552 | tf_op jit(solution)/shard_map/all_to_all | solution.py:27
  28.8 1.0 reshape.20
  29.7 0.0 copy-start
  29.7 1.5 %copy.17 = bf16[2,32,8,480]{3,0,2,1:T(2,128)(2,1)S(1)} copy(bf16[2,32,8,480]{1,0,3,2:T(2,128)(2,1)S(1)} %bitcast.17) | data formatting | bytes 983040 | tf_op jit(solution)/shard_map/all_to_all | solution.py:27
  31.3 0.0 copy-start.1
  31.3 0.4 all_to_all.16
  31.7 0.0 copy-done
  31.7 1.1 multiply_reduce_fusion
  32.8 1.1 copy.19
  33.9 35.0 %psum.21 = f32[32]{0:T(128)S(1)} all-reduce(f32[32]{0:T(128)S(1)} %broadcast_multiply_fusion), channel_id=1, replica_groups=mesh['row'=8,'col'=8,'tm'=8] {'col'}, use_global_device_ids=true, to_apply=%region_1.0 | all-reduce | flops 32 | bytes 256 | tf_op jit(solution)/shard_map/psum | solution.py:35
  68.9 15.6 %psum.22 = f32[32]{0:T(128)S(1)} all-reduce(f32[32]{0:T(128)S(1)} %psum.21), channel_id=1, replica_groups=mesh['row'=8,'col'=8,'tm'=8] {'tm'}, use_global_device_ids=true, to_apply=%region_2.0 | all-reduce | flops 32 | bytes 256 | tf_op jit(solution)/shard_map/psum | solution.py:35
  84.6 0.0 copy-done.1
  84.6 0.2 fusion
  84.8 26.5 %psum.23 = f32[3,1000]{1,0:T(4,128)} all-reduce(f32[3,1000]{1,0:T(4,128)S(1)} %fusion), channel_id=1, replica_groups=mesh['row'=8,'col'=8,'tm'=8] {'row'}, use_global_device_ids=true, to_apply=%region_3.0 | all-reduce | flops 3000 | bytes 24000 | tf_op jit(solution)/shard_map/psum | solution.py:42
  (2 shorter events, 0.0 us)
Async XLA Ops:
  5.9 22.9 %all-to-all-start = ((bf16[8,2,15360]{2,1,0:T(2,128)(2,1)}), bf16[8,2,15360]{2,1,0:T(2,128)(2,1)S(1)}, u32[]{:S(2)}, u32[]{:S(2)}) async-start(bf16[8,2,15360]{2,1,0:T(2,128)(2,1)} %reshape.19), calls=%async_computation | async-start | bytes 983040 | tf_op jit(solution)/shard_map/all_to_all | solution.py:27
  29.7 2.0 %copy-start = (bf16[16,32,480]{2,1,0:T(8,128)(2,1)S(1)}, bf16[16,32,480]{2,1,0:T(8,128)(2,1)}, u32[]{:S(2)}) copy-start(bf16[16,32,480]{2,1,0:T(8,128)(2,1)} %param.8) | copy-start | bytes 1474564
  31.3 53.3 %copy-start.1 = (f32[3,32]{1,0:T(4,128)S(1)}, f32[3,32]{1,0:T(4,128)}, u32[]{:S(2)}) copy-start(f32[3,32]{1,0:T(4,128)} %param.9) | copy-start | bytes 1156

commit v2 on v0

--- a/solution.py
+++ b/solution.py
@@ -39,7 +39,7 @@
         precision=lax.Precision.HIGHEST,
         preferred_element_type=jnp.float32,
     )
-    forces = lax.psum(local_forces, "row")
+    forces = jnp.sum(lax.all_gather(local_forces, "row"), axis=0)
     return (chi_freq, forces)
 
 

time: 283 us -> 275 us (0.972)
  blocking collectives: 250 us -> 242 us
    psum x1 -> x0, blocking collectives: 53.3 us -> none  [on_device(): forces = lax.psum(local_forces, 'row')]
    all_gather x0 -> x1, blocking collectives: none -> 45.3 us  [on_device(): forces = jnp.sum(lax.all_gather(local_forces, 'row'), axis=0)]
where the time goes in v2:
time: 275 us
  blocking collectives  242 us (88%)
  waiting for transfers between devices  12.4 us (5%)
  local copies, waits for them, and re-layouts  8.71 us (3%)
  starting transfers between devices  7.65 us (3%)
    psum x1, blocking collectives, on_device(): energy = lax.psum(partial_value, ('col', 'tm'))  196 us
    all_gather x1, blocking collectives, on_device(): forces = jnp.sum(lax.all_gather(local_forces, 'row'), axis=0)  45.3 us
    all_to_all x1, waiting for transfers between devices, on_device(): lax.all_to_all(product, 'tm', split_axis=2, concat_axis=0, tiled=True)  12.4 us
    all_to_all x1, starting transfers between devices, on_device(): lax.all_to_all(product, 'tm', split_axis=2, concat_axis=0, tiled=True)  7.65 us
  transfers between devices with their start and end apart: 1, of which 1 were waited for; matrix products, arithmetic and copies ran while one was open for 0% of the time, Pallas kernels for 0%

profile of v2, /device:TPU:1, one launch (start us, length us, event | category | flops | bytes accessed | tf_op | source)
XLA Modules:
  0.0 275.1 jit_solution(2470787601660696427)
XLA Ops:
  0.6 1.3 multiply_convert_fusion
  1.9 1.4 copy.16
  3.3 2.5 reshape.23
  5.9 7.7 %all-to-all-start = ((bf16[8,2,15360]{2,1,0:T(2,128)(2,1)}), bf16[8,2,15360]{2,1,0:T(2,128)(2,1)S(1)}, u32[]{:S(2)}, u32[]{:S(2)}) async-start(bf16[8,2,15360]{2,1,0:T(2,128)(2,1)} %reshape.23), calls=%async_computation | async-start | bytes 983040 | tf_op jit(solution)/shard_map/all_to_all | solution.py:27
  14.2 0.8 dynamic_slice.3
  15.0 12.4 %all-to-all-done = bf16[8,2,15360]{2,1,0:T(2,128)(2,1)S(1)} async-done(((bf16[8,2,15360]{2,1,0:T(2,128)(2,1)}), bf16[8,2,15360]{2,1,0:T(2,128)(2,1)S(1)}, u32[]{:S(2)}, u32[]{:S(2)}) %all-to-all-start) | async-done | bytes 491552 | tf_op jit(solution)/shard_map/all_to_all | solution.py:27
  27.4 1.0 reshape.24
  28.4 0.0 copy-start
  28.4 1.5 copy.17
  29.9 0.0 copy-start.1
  29.9 0.4 all_to_all.16
  30.3 0.0 copy-done
  30.4 1.1 multiply_reduce_fusion
  31.5 1.1 copy.19
  32.5 196.4 %psum.7 = f32[32]{0:T(128)S(1)} all-reduce(f32[32]{0:T(128)S(1)} %broadcast_multiply_fusion), channel_id=1, replica_groups=mesh['row'=8,'col'=8,'tm'=8] {'col','tm'}, use_global_device_ids=true, to_apply=%region_1.0 | all-reduce | flops 32 | bytes 256 | tf_op jit(solution)/shard_map/psum | solution.py:35
  228.9 0.0 copy-done.1
  228.9 0.2 convolution_bitcast_fusion
  229.1 45.3 %all-gather.1 = f32[8,3,1000]{2,1,0:T(4,128)S(1)} all-gather(f32[1,3,1000]{2,1,0:T(4,128)S(1)} %convolution_bitcast_fusion), channel_id=2, replica_groups=mesh['row'=8,'col'=8,'tm'=8] {'row'}, dimensions={0}, use_global_device_ids=true | all-gather | bytes 108000 | tf_op jit(solution)/shard_map/all_gather | solution.py:42
  274.5 0.6 reduce_sum.19
  (2 shorter events, 0.0 us)
Async XLA Ops:
  5.9 21.5 %all-to-all-start = ((bf16[8,2,15360]{2,1,0:T(2,128)(2,1)}), bf16[8,2,15360]{2,1,0:T(2,128)(2,1)S(1)}, u32[]{:S(2)}, u32[]{:S(2)}) async-start(bf16[8,2,15360]{2,1,0:T(2,128)(2,1)} %reshape.23), calls=%async_computation | async-start | bytes 983040 | tf_op jit(solution)/shard_map/all_to_all | solution.py:27
  28.4 2.0 copy-start
  29.9 199.0 %copy-start.1 = (f32[3,32]{1,0:T(4,128)S(1)}, f32[3,32]{1,0:T(4,128)}, u32[]{:S(2)}) copy-start(f32[3,32]{1,0:T(4,128)} %param.9) | copy-start | bytes 1156
